TPU v7x, 512 devices: a whole 4x4x16 slice. The times are simulated.
512 devices in a mesh: blk: 32 (over y, z_hi, core), sub: 16 (over z_lo, x).
Axes of the slice: x: 4, y: 4, z: 16 (z_hi: 4, z_lo: 4; z = z_hi * 4 + z_lo), core: 2. Of those that a mesh axis runs over, the one named last changes fastest.
Arguments:
- features: float32 [16384, 512], P(('blk', 'sub')), may hold values from -3 to 3
- lengthscale: float32 [512], replicated, may hold values from 0.7 to 1.4
- probes: float32 [16384, 64], P(('blk', 'sub')), may hold values from -6 to 6
- cotangent: float32 [16384, 64], P(('blk', 'sub')), may hold values from -1.5 to 1.5
Outputs:
- product: float32 [16384, 64], P(('blk', 'sub'))
- scaled_grad: float32 [16384, 512], P(('blk', 'sub'))
All inputs are finite; a program needn't handle non-finite values.
Results may differ from a plain program's by a relative error of at most 0.0003.
Values sent between devices are 32-bit elements; how exact they have to be, the bound alone decides.
A program may use at most 64 MiB of HBM per device.

v0:
```python
import math

import jax
import jax.numpy as jnp
from jax import lax
from jax.sharding import PartitionSpec as P

HIGH = lax.Precision.HIGHEST
ROWS_RULE = (((1,), (1,)), ((), ()))
COLS_RULE = (((0,), (0,)), ((), ()))


def passed_along(value, axis, by):
    length = lax.axis_size(axis)
    return lax.ppermute(value, axis, [(i, (i + by) % length) for i in range(length)])


def from_everyone(value, axis):
    length = lax.axis_size(axis)
    return lax.all_to_all(
        jnp.broadcast_to(value[None], (length, *value.shape)), axis, 0, 0, tiled=True
    )


def joined_along(tiles, dim):
    shape = list(tiles.shape[1:])
    shape[dim] *= tiles.shape[0]
    return jnp.moveaxis(tiles, 0, dim).reshape(shape)


def collect(value, axis, dim):
    tiles = from_everyone(value, axis)
    return joined_along(tiles, dim)


def sent_together(arrays, axis, dim, along):
    widths = [math.prod(a.shape[along:]) for a in arrays]
    both = jnp.concatenate(
        [a.reshape(*a.shape[:along], w) for a, w in zip(arrays, widths)], axis=along
    )
    filled = collect(both, axis, dim)
    tiles = jnp.split(filled, [sum(widths[:k]) for k in range(1, len(widths))], axis=along)
    return tuple(
        (b.reshape(*filled.shape[:along], *a.shape[along:]) for a, b in zip(arrays, tiles))
    )


def split_up(value, dim, length):
    before, after = (value.shape[:dim], value.shape[dim + 1 :])
    return jnp.moveaxis(value.reshape(*before, length, -1, *after), dim, 0)


def sent_and_summed(value, axis, dim):
    length = lax.axis_size(axis)
    tiles = lax.all_to_all(split_up(value, dim, length), axis, 0, 0, tiled=True)
    return jnp.sum(tiles, axis=0)


def side_by_side(arrays, axis, dim, along):
    both = jnp.concatenate(arrays, axis=along)
    filled, at, finished = (sent_and_summed(both, axis, dim), 0, [])
    for a in arrays:
        finished.append(lax.slice_in_dim(filled, at, at + a.shape[along], axis=along))
        at += a.shape[along]
    return tuple(finished)


def pair_terms(home_scaled, home_pair, home_norms, away_scaled, away_pair, away_norms):
    middle = away_pair.shape[1] // 2
    inner = lax.dot_general(
        home_scaled, away_scaled, ROWS_RULE, precision=HIGH, preferred_element_type=jnp.float32
    )
    kernel = jnp.exp(-0.5 * (home_norms[:, None] + away_norms[None, :] - 2.0 * inner))
    swapped = jnp.concatenate([away_pair[:, middle:], away_pair[:, :middle]], axis=1)
    cross = lax.dot_general(
        home_pair, swapped, ROWS_RULE, precision=HIGH, preferred_element_type=jnp.float32
    )
    return (kernel, kernel * cross)


def resident_side(kernel, weight, home_scaled, away_scaled, away_pair):
    middle = away_pair.shape[1] // 2
    product = jnp.dot(
        kernel, away_pair[:, :middle], precision=HIGH, preferred_element_type=jnp.float32
    )
    gradient = jnp.dot(weight, away_scaled, precision=HIGH, preferred_element_type=jnp.float32)
    return (product, gradient - jnp.sum(weight, axis=1)[:, None] * home_scaled)


def travel_side(kernel, weight, home_scaled, home_pair, away_scaled):
    middle = home_pair.shape[1] // 2
    product = lax.dot_general(
        kernel, home_pair[:, :middle], COLS_RULE, precision=HIGH, preferred_element_type=jnp.float32
    )
    gradient = lax.dot_general(
        weight, home_scaled, COLS_RULE, precision=HIGH, preferred_element_type=jnp.float32
    )
    return (product, gradient - jnp.sum(weight, axis=0)[:, None] * away_scaled)


def advance(away_scaled, away_pair, away_norms, away_product, away_gradient):
    return passed_along((away_scaled, away_pair, away_norms, away_product, away_gradient), "blk", 1)


def on_device(features, lengthscale, probes, cotangent):
    scaled = features / lengthscale[None, :]
    pairs = jnp.concatenate([probes, cotangent], axis=1)
    norms = jnp.sum(scaled * scaled, axis=1)
    home_scaled, home_pair, home_norms = sent_together((scaled, pairs, norms), "sub", 0, 1)
    kernel, weight = pair_terms(home_scaled, home_pair, home_norms, scaled, pairs, norms)
    home_product, home_gradient = resident_side(kernel, weight, home_scaled, scaled, pairs)
    blocks = lax.axis_size("blk")
    middle = blocks // 2

    def step_two(offset, running):
        moved = advance(running[0], running[1], running[2], running[3], running[4])
        kernel_now, weight_now = pair_terms(
            home_scaled, home_pair, home_norms, moved[0], moved[1], moved[2]
        )
        near_product, near_gradient = resident_side(
            kernel_now, weight_now, home_scaled, moved[0], moved[1]
        )
        far_product, far_gradient = travel_side(
            kernel_now, weight_now, home_scaled, home_pair, moved[0]
        )
        return (
            moved[0],
            moved[1],
            moved[2],
            moved[3] + far_product,
            moved[4] + far_gradient,
            running[5] + near_product,
            running[6] + near_gradient,
        )

    start = (
        scaled,
        pairs,
        norms,
        jnp.zeros(probes.shape, jnp.float32),
        jnp.zeros(features.shape, jnp.float32),
        home_product,
        home_gradient,
    )
    running = lax.fori_loop(1, middle, step_two, start)
    moved = advance(running[0], running[1], running[2], running[3], running[4])
    kernel_last, weight_last = pair_terms(
        home_scaled, home_pair, home_norms, moved[0], moved[1], moved[2]
    )
    last_product, last_gradient = resident_side(
        kernel_last, weight_last, home_scaled, moved[0], moved[1]
    )
    home_product = running[5] + last_product
    home_gradient = running[6] + last_gradient
    back_product, back_gradient = passed_along((moved[3], moved[4]), "blk", middle)
    own_product, own_gradient = side_by_side((home_product, home_gradient), "sub", 0, 1)
    return (own_product + back_product, own_gradient + back_gradient)


def solution(mesh):
    in_specs = (P(("blk", "sub"), None), P(), P(("blk", "sub"), None), P(("blk", "sub"), None))
    out_specs = (P(("blk", "sub"), None), P(("blk", "sub"), None))
    return jax.shard_map(
        on_device, mesh=mesh, in_specs=in_specs, out_specs=out_specs, check_vma=False
    )
```

profile of v0, /device:TPU:34, one launch (start us, length us, event | category | flops | bytes accessed | tf_op | source)
XLA Modules:
  0.0 578.9 jit_solution(12451526138438873620)
XLA Ops:
  3.8 9.1 %all-to-all-start = ((f32[16,32,641]{2,1,0:T(8,128)}), f32[16,32,641]{2,1,0:T(8,128)S(1)}, u32[]{:S(2)}, u32[]{:S(2)}) async-start(f32[16,32,641]{2,1,0:T(8,128)} %broadcast_in_dim.8), calls=%async_computation | async-start | bytes 3145728 | tf_op jit(solution)/shard_map/all_to_all | solution.py:20
  13.0 34.8 %all-to-all-done = f32[16,32,641]{2,1,0:T(8,128)S(1)} async-done(((f32[16,32,641]{2,1,0:T(8,128)}), f32[16,32,641]{2,1,0:T(8,128)S(1)}, u32[]{:S(2)}, u32[]{:S(2)}) %all-to-all-start) | async-done | bytes 1312800 | tf_op jit(solution)/shard_map/all_to_all | solution.py:20
  53.5 441.0 %while.23 = (s32[]{:T(128)}, f32[32,512]{1,0:T(8,128)S(1)}, f32[32,128]{1,0:T(8,128)S(1)}, f32[32]{0:T(128)S(1)}, f32[32,64]{1,0:T(8,128)S(1)}, /*index=5*/f32[3...) while((s32[]{:T(128)}, f32[32,512]{1,0:T(8,128)S(1)}, ...), condition=%wide.region_5.0_spmd.clone, body=%wide.region_2.0_spmd.clone.sunk | while | flops 353426912 | bytes 7843536 | solution.py:145
  55.5 9.2 %collective-permute-start.3 = (f32[32,64]{1,0:T(8,128)S(1)}, f32[32,64]{1,0:T(8,128)S(1)}, u32[]{:S(2)}, u32[]{:S(2)}) collective-permute-start(f32[32,64]{1,0:T(8,128)S(1)} %broadcast_select_fusion.4), channel_id=1, source_target_pairs={{0,16},{16,32},{32,48},{48,64},{64,80},{80,96},{96,112},{112,128},... | collective-permute-start | bytes 24584 | tf_op jit(solution)/shard_map/while/body/eval_jaxpr/ppermute | solution.py:15
  66.7 6.4 %collective-permute-start.4 = (f32[32,512]{1,0:T(8,128)S(1)}, f32[32,512]{1,0:T(8,128)S(1)}, u32[]{:S(2)}, u32[]{:S(2)}) collective-permute-start(f32[32,512]{1,0:T(8,128)S(1)} %broadcast_select_fusion.5), channel_id=1, source_target_pairs={{0,16},{16,32},{32,48},{48,64},{64,80},{80,96},{96,112},{112,128},... | collective-permute-start | bytes 196616 | tf_op jit(solution)/shard_map/while/body/eval_jaxpr/ppermute | solution.py:15
  75.9 8.8 %collective-permute-done = f32[32,512]{1,0:T(8,128)S(1)} collective-permute-done((f32[32,512]{1,0:T(8,128)S(1)}, f32[32,512]{1,0:T(8,128)S(1)}, u32[]{:S(2)}, u32[]{:S(2)}) %collective-permute-start) | collective-permute-done | bytes 65568 | tf_op jit(solution)/shard_map/while/body/eval_jaxpr/ppermute | solution.py:15
  100.2 4.2 collective-permute-done.1
  104.5 4.4 collective-permute-done
  115.2 8.1 %collective-permute-start.3 = (f32[32,64]{1,0:T(8,128)S(1)}, f32[32,64]{1,0:T(8,128)S(1)}, u32[]{:S(2)}, u32[]{:S(2)}) collective-permute-start(f32[32,64]{1,0:T(8,128)S(1)} %broadcast_select_fusion.4), channel_id=1, source_target_pairs={{0,16},{16,32},{32,48},{48,64},{64,80},{80,96},{96,112},{112,128},... | collective-permute-start | bytes 24584 | tf_op jit(solution)/shard_map/while/body/eval_jaxpr/ppermute | solution.py:15
  125.3 5.1 collective-permute-start.4
  134.6 7.4 %collective-permute-done = f32[32,512]{1,0:T(8,128)S(1)} collective-permute-done((f32[32,512]{1,0:T(8,128)S(1)}, f32[32,512]{1,0:T(8,128)S(1)}, u32[]{:S(2)}, u32[]{:S(2)}) %collective-permute-start) | collective-permute-done | bytes 65568 | tf_op jit(solution)/shard_map/while/body/eval_jaxpr/ppermute | solution.py:15
  161.6 6.7 %collective-permute-done = f32[32,512]{1,0:T(8,128)S(1)} collective-permute-done((f32[32,512]{1,0:T(8,128)S(1)}, f32[32,512]{1,0:T(8,128)S(1)}, u32[]{:S(2)}, u32[]{:S(2)}) %collective-permute-start) | collective-permute-done | bytes 65568 | tf_op jit(solution)/shard_map/while/body/eval_jaxpr/ppermute | solution.py:15
  174.6 7.7 %collective-permute-start.3 = (f32[32,64]{1,0:T(8,128)S(1)}, f32[32,64]{1,0:T(8,128)S(1)}, u32[]{:S(2)}, u32[]{:S(2)}) collective-permute-start(f32[32,64]{1,0:T(8,128)S(1)} %broadcast_select_fusion.4), channel_id=1, source_target_pairs={{0,16},{16,32},{32,48},{48,64},{64,80},{80,96},{96,112},{112,128},... | collective-permute-start | bytes 24584 | tf_op jit(solution)/shard_map/while/body/eval_jaxpr/ppermute | solution.py:15
  189.6 4.1 collective-permute-done.1
  193.9 5.4 collective-permute-done
  209.4 3.8 collective-permute-start.4
  213.2 3.9 collective-permute-start
  218.6 6.7 %collective-permute-done = f32[32,512]{1,0:T(8,128)S(1)} collective-permute-done((f32[32,512]{1,0:T(8,128)S(1)}, f32[32,512]{1,0:T(8,128)S(1)}, u32[]{:S(2)}, u32[]{:S(2)}) %collective-permute-start) | collective-permute-done | bytes 65568 | tf_op jit(solution)/shard_map/while/body/eval_jaxpr/ppermute | solution.py:15
  232.5 8.3 %collective-permute-start.3 = (f32[32,64]{1,0:T(8,128)S(1)}, f32[32,64]{1,0:T(8,128)S(1)}, u32[]{:S(2)}, u32[]{:S(2)}) collective-permute-start(f32[32,64]{1,0:T(8,128)S(1)} %broadcast_select_fusion.4), channel_id=1, source_target_pairs={{0,16},{16,32},{32,48},{48,64},{64,80},{80,96},{96,112},{112,128},... | collective-permute-start | bytes 24584 | tf_op jit(solution)/shard_map/while/body/eval_jaxpr/ppermute | solution.py:15
  247.5 4.4 collective-permute-done.1
  251.9 6.6 %collective-permute-done = f32[32,512]{1,0:T(8,128)S(1)} collective-permute-done((f32[32,512]{1,0:T(8,128)S(1)}, f32[32,512]{1,0:T(8,128)S(1)}, u32[]{:S(2)}, u32[]{:S(2)}) %collective-permute-start) | collective-permute-done | bytes 65568 | tf_op jit(solution)/shard_map/while/body/eval_jaxpr/ppermute | solution.py:15
  268.7 4.7 collective-permute-start.4
  277.9 7.3 %collective-permute-done = f32[32,512]{1,0:T(8,128)S(1)} collective-permute-done((f32[32,512]{1,0:T(8,128)S(1)}, f32[32,512]{1,0:T(8,128)S(1)}, u32[]{:S(2)}, u32[]{:S(2)}) %collective-permute-start) | collective-permute-done | bytes 65568 | tf_op jit(solution)/shard_map/while/body/eval_jaxpr/ppermute | solution.py:15
  296.1 8.2 %collective-permute-start.4 = (f32[32,512]{1,0:T(8,128)S(1)}, f32[32,512]{1,0:T(8,128)S(1)}, u32[]{:S(2)}, u32[]{:S(2)}) collective-permute-start(f32[32,512]{1,0:T(8,128)S(1)} %broadcast_select_fusion.5), channel_id=1, source_target_pairs={{0,16},{16,32},{32,48},{48,64},{64,80},{80,96},{96,112},{112,128},... | collective-permute-start | bytes 196616 | tf_op jit(solution)/shard_map/while/body/eval_jaxpr/ppermute | solution.py:15
  306.3 11.5 %collective-permute-done = f32[32,512]{1,0:T(8,128)S(1)} collective-permute-done((f32[32,512]{1,0:T(8,128)S(1)}, f32[32,512]{1,0:T(8,128)S(1)}, u32[]{:S(2)}, u32[]{:S(2)}) %collective-permute-start) | collective-permute-done | bytes 65568 | tf_op jit(solution)/shard_map/while/body/eval_jaxpr/ppermute | solution.py:15
  333.0 4.0 collective-permute-done.1
  337.1 4.7 collective-permute-done
  348.1 6.9 %collective-permute-start.3 = (f32[32,64]{1,0:T(8,128)S(1)}, f32[32,64]{1,0:T(8,128)S(1)}, u32[]{:S(2)}, u32[]{:S(2)}) collective-permute-start(f32[32,64]{1,0:T(8,128)S(1)} %broadcast_select_fusion.4), channel_id=1, source_target_pairs={{0,16},{16,32},{32,48},{48,64},{64,80},{80,96},{96,112},{112,128},... | collective-permute-start | bytes 24584 | tf_op jit(solution)/shard_map/while/body/eval_jaxpr/ppermute | solution.py:15
  357.0 4.2 collective-permute-start.4
  366.2 7.7 %collective-permute-done = f32[32,512]{1,0:T(8,128)S(1)} collective-permute-done((f32[32,512]{1,0:T(8,128)S(1)}, f32[32,512]{1,0:T(8,128)S(1)}, u32[]{:S(2)}, u32[]{:S(2)}) %collective-permute-start) | collective-permute-done | bytes 65568 | tf_op jit(solution)/shard_map/while/body/eval_jaxpr/ppermute | solution.py:15
  384.1 8.0 %collective-permute-start.4 = (f32[32,512]{1,0:T(8,128)S(1)}, f32[32,512]{1,0:T(8,128)S(1)}, u32[]{:S(2)}, u32[]{:S(2)}) collective-permute-start(f32[32,512]{1,0:T(8,128)S(1)} %broadcast_select_fusion.5), channel_id=1, source_target_pairs={{0,16},{16,32},{32,48},{48,64},{64,80},{80,96},{96,112},{112,128},... | collective-permute-start | bytes 196616 | tf_op jit(solution)/shard_map/while/body/eval_jaxpr/ppermute | solution.py:15
  394.1 12.2 %collective-permute-done = f32[32,512]{1,0:T(8,128)S(1)} collective-permute-done((f32[32,512]{1,0:T(8,128)S(1)}, f32[32,512]{1,0:T(8,128)S(1)}, u32[]{:S(2)}, u32[]{:S(2)}) %collective-permute-start) | collective-permute-done | bytes 65568 | tf_op jit(solution)/shard_map/while/body/eval_jaxpr/ppermute | solution.py:15
  421.5 4.0 collective-permute-done.1
  425.6 4.9 collective-permute-done
  440.6 4.1 collective-permute-start.4
  444.7 5.1 collective-permute-start
  450.3 6.2 %collective-permute-done = f32[32,512]{1,0:T(8,128)S(1)} collective-permute-done((f32[32,512]{1,0:T(8,128)S(1)}, f32[32,512]{1,0:T(8,128)S(1)}, u32[]{:S(2)}, u32[]{:S(2)}) %collective-permute-start) | collective-permute-done | bytes 65568 | tf_op jit(solution)/shard_map/while/body/eval_jaxpr/ppermute | solution.py:15
  460.8 4.7 collective-permute-start.2
  465.5 8.3 %collective-permute-start.3 = (f32[32,64]{1,0:T(8,128)S(1)}, f32[32,64]{1,0:T(8,128)S(1)}, u32[]{:S(2)}, u32[]{:S(2)}) collective-permute-start(f32[32,64]{1,0:T(8,128)S(1)} %broadcast_select_fusion.4), channel_id=1, source_target_pairs={{0,16},{16,32},{32,48},{48,64},{64,80},{80,96},{96,112},{112,128},... | collective-permute-start | bytes 24584 | tf_op jit(solution)/shard_map/while/body/eval_jaxpr/ppermute | solution.py:15
  479.7 5.3 collective-permute-done.1
  485.0 5.2 collective-permute-done
  500.3 5.3 collective-permute-done.7
  505.7 4.3 collective-permute-done.6
  517.9 9.6 %all-to-all-start.1 = ((f32[16,32,576]{2,1,0:T(8,128)}), f32[16,32,576]{2,1,0:T(8,128)S(1)}, u32[]{:S(2)}, u32[]{:S(2)}) async-start(f32[16,32,576]{2,1,0:T(8,128)} %bitcast.2), calls=%async_computation.1 | async-start | bytes 2621440 | tf_op jit(solution)/shard_map/all_to_all | solution.py:55
  529.4 26.4 %collective-permute-done.10 = f32[32,512]{1,0:T(8,128)S(1)} collective-permute-done((f32[32,512]{1,0:T(8,128)S(1)}, f32[32,512]{1,0:T(8,128)S(1)}, u32[]{:S(2)}, u32[]{:S(2)}) %collective-permute-start.10) | collective-permute-done | bytes 65568 | tf_op jit(solution)/shard_map/ppermute | solution.py:15
  555.8 4.3 collective-permute-start.11
  562.0 9.1 %collective-permute-done.8 = f32[32,64]{1,0:T(8,128)S(1)} collective-permute-done((f32[32,64]{1,0:T(8,128)S(1)}, f32[32,64]{1,0:T(8,128)S(1)}, u32[]{:S(2)}, u32[]{:S(2)}) %collective-permute-start.8) | collective-permute-done | bytes 8224 | tf_op jit(solution)/shard_map/ppermute | solution.py:15
  573.9 4.4 collective-permute-done.9
  (332 shorter events, 229.9 us)
Async XLA Ops:
  3.8 44.0 %all-to-all-start = ((f32[16,32,641]{2,1,0:T(8,128)}), f32[16,32,641]{2,1,0:T(8,128)S(1)}, u32[]{:S(2)}, u32[]{:S(2)}) async-start(f32[16,32,641]{2,1,0:T(8,128)} %broadcast_in_dim.8), calls=%async_computation | async-start | bytes 3145728 | tf_op jit(solution)/shard_map/all_to_all | solution.py:20
  53.5 21.5 %collective-permute-start.2 = (f32[32]{0:T(128)S(1)}, f32[32]{0:T(128)S(1)}, u32[]{:S(2)}, u32[]{:S(2)}) collective-permute-start(f32[32]{0:T(128)S(1)} %get-tuple-element.271), channel_id=1, source_target_pairs={{0,16},{16,32},{32,48},{48,64},{64,80},{80,96},{96,112},{112,128},... | collective-permute-start | bytes 392 | tf_op jit(solution)/shard_map/while/body/eval_jaxpr/ppermute | solution.py:15
  55.5 30.3 %collective-permute-start.3 = (f32[32,64]{1,0:T(8,128)S(1)}, f32[32,64]{1,0:T(8,128)S(1)}, u32[]{:S(2)}, u32[]{:S(2)}) collective-permute-start(f32[32,64]{1,0:T(8,128)S(1)} %broadcast_select_fusion.4), channel_id=1, source_target_pairs={{0,16},{16,32},{32,48},{48,64},{64,80},{80,96},{96,112},{112,128},... | collective-permute-start | bytes 24584 | tf_op jit(solution)/shard_map/while/body/eval_jaxpr/ppermute | solution.py:15
  66.7 20.4 %collective-permute-start.4 = (f32[32,512]{1,0:T(8,128)S(1)}, f32[32,512]{1,0:T(8,128)S(1)}, u32[]{:S(2)}, u32[]{:S(2)}) collective-permute-start(f32[32,512]{1,0:T(8,128)S(1)} %broadcast_select_fusion.5), channel_id=1, source_target_pairs={{0,16},{16,32},{32,48},{48,64},{64,80},{80,96},{96,112},{112,128},... | collective-permute-start | bytes 196616 | tf_op jit(solution)/shard_map/while/body/eval_jaxpr/ppermute | solution.py:15
  91.0 19.0 %collective-permute-start.3 = (f32[32,64]{1,0:T(8,128)S(1)}, f32[32,64]{1,0:T(8,128)S(1)}, u32[]{:S(2)}, u32[]{:S(2)}) collective-permute-start(f32[32,64]{1,0:T(8,128)S(1)} %broadcast_select_fusion.4), channel_id=1, source_target_pairs={{0,16},{16,32},{32,48},{48,64},{64,80},{80,96},{96,112},{112,128},... | collective-permute-start | bytes 24584 | tf_op jit(solution)/shard_map/while/body/eval_jaxpr/ppermute | solution.py:15
  95.3 16.0 %collective-permute-start.4 = (f32[32,512]{1,0:T(8,128)S(1)}, f32[32,512]{1,0:T(8,128)S(1)}, u32[]{:S(2)}, u32[]{:S(2)}) collective-permute-start(f32[32,512]{1,0:T(8,128)S(1)} %broadcast_select_fusion.5), channel_id=1, source_target_pairs={{0,16},{16,32},{32,48},{48,64},{64,80},{80,96},{96,112},{112,128},... | collective-permute-start | bytes 196616 | tf_op jit(solution)/shard_map/while/body/eval_jaxpr/ppermute | solution.py:15
  113.3 19.1 %collective-permute-start.2 = (f32[32]{0:T(128)S(1)}, f32[32]{0:T(128)S(1)}, u32[]{:S(2)}, u32[]{:S(2)}) collective-permute-start(f32[32]{0:T(128)S(1)} %get-tuple-element.271), channel_id=1, source_target_pairs={{0,16},{16,32},{32,48},{48,64},{64,80},{80,96},{96,112},{112,128},... | collective-permute-start | bytes 392 | tf_op jit(solution)/shard_map/while/body/eval_jaxpr/ppermute | solution.py:15
  115.2 27.9 %collective-permute-start.3 = (f32[32,64]{1,0:T(8,128)S(1)}, f32[32,64]{1,0:T(8,128)S(1)}, u32[]{:S(2)}, u32[]{:S(2)}) collective-permute-start(f32[32,64]{1,0:T(8,128)S(1)} %broadcast_select_fusion.4), channel_id=1, source_target_pairs={{0,16},{16,32},{32,48},{48,64},{64,80},{80,96},{96,112},{112,128},... | collective-permute-start | bytes 24584 | tf_op jit(solution)/shard_map/while/body/eval_jaxpr/ppermute | solution.py:15
  125.3 19.0 %collective-permute-start.4 = (f32[32,512]{1,0:T(8,128)S(1)}, f32[32,512]{1,0:T(8,128)S(1)}, u32[]{:S(2)}, u32[]{:S(2)}) collective-permute-start(f32[32,512]{1,0:T(8,128)S(1)} %broadcast_select_fusion.5), channel_id=1, source_target_pairs={{0,16},{16,32},{32,48},{48,64},{64,80},{80,96},{96,112},{112,128},... | collective-permute-start | bytes 196616 | tf_op jit(solution)/shard_map/while/body/eval_jaxpr/ppermute | solution.py:15
  148.3 21.1 %collective-permute-start.3 = (f32[32,64]{1,0:T(8,128)S(1)}, f32[32,64]{1,0:T(8,128)S(1)}, u32[]{:S(2)}, u32[]{:S(2)}) collective-permute-start(f32[32,64]{1,0:T(8,128)S(1)} %broadcast_select_fusion.4), channel_id=1, source_target_pairs={{0,16},{16,32},{32,48},{48,64},{64,80},{80,96},{96,112},{112,128},... | collective-permute-start | bytes 24584 | tf_op jit(solution)/shard_map/while/body/eval_jaxpr/ppermute | solution.py:15
  152.4 18.2 %collective-permute-start.4 = (f32[32,512]{1,0:T(8,128)S(1)}, f32[32,512]{1,0:T(8,128)S(1)}, u32[]{:S(2)}, u32[]{:S(2)}) collective-permute-start(f32[32,512]{1,0:T(8,128)S(1)} %broadcast_select_fusion.5), channel_id=1, source_target_pairs={{0,16},{16,32},{32,48},{48,64},{64,80},{80,96},{96,112},{112,128},... | collective-permute-start | bytes 196616 | tf_op jit(solution)/shard_map/while/body/eval_jaxpr/ppermute | solution.py:15
  172.6 17.0 %collective-permute-start.2 = (f32[32]{0:T(128)S(1)}, f32[32]{0:T(128)S(1)}, u32[]{:S(2)}, u32[]{:S(2)}) collective-permute-start(f32[32]{0:T(128)S(1)} %get-tuple-element.271), channel_id=1, source_target_pairs={{0,16},{16,32},{32,48},{48,64},{64,80},{80,96},{96,112},{112,128},... | collective-permute-start | bytes 392 | tf_op jit(solution)/shard_map/while/body/eval_jaxpr/ppermute | solution.py:15
  174.6 25.8 %collective-permute-start.3 = (f32[32,64]{1,0:T(8,128)S(1)}, f32[32,64]{1,0:T(8,128)S(1)}, u32[]{:S(2)}, u32[]{:S(2)}) collective-permute-start(f32[32,64]{1,0:T(8,128)S(1)} %broadcast_select_fusion.4), channel_id=1, source_target_pairs={{0,16},{16,32},{32,48},{48,64},{64,80},{80,96},{96,112},{112,128},... | collective-permute-start | bytes 24584 | tf_op jit(solution)/shard_map/while/body/eval_jaxpr/ppermute | solution.py:15
  184.2 17.4 %collective-permute-start.4 = (f32[32,512]{1,0:T(8,128)S(1)}, f32[32,512]{1,0:T(8,128)S(1)}, u32[]{:S(2)}, u32[]{:S(2)}) collective-permute-start(f32[32,512]{1,0:T(8,128)S(1)} %broadcast_select_fusion.5), channel_id=1, source_target_pairs={{0,16},{16,32},{32,48},{48,64},{64,80},{80,96},{96,112},{112,128},... | collective-permute-start | bytes 196616 | tf_op jit(solution)/shard_map/while/body/eval_jaxpr/ppermute | solution.py:15
  203.6 13.5 %collective-permute-start.2 = (f32[32]{0:T(128)S(1)}, f32[32]{0:T(128)S(1)}, u32[]{:S(2)}, u32[]{:S(2)}) collective-permute-start(f32[32]{0:T(128)S(1)} %get-tuple-element.271), channel_id=1, source_target_pairs={{0,16},{16,32},{32,48},{48,64},{64,80},{80,96},{96,112},{112,128},... | collective-permute-start | bytes 392 | tf_op jit(solution)/shard_map/while/body/eval_jaxpr/ppermute | solution.py:15
  205.6 20.8 %collective-permute-start.3 = (f32[32,64]{1,0:T(8,128)S(1)}, f32[32,64]{1,0:T(8,128)S(1)}, u32[]{:S(2)}, u32[]{:S(2)}) collective-permute-start(f32[32,64]{1,0:T(8,128)S(1)} %broadcast_select_fusion.4), channel_id=1, source_target_pairs={{0,16},{16,32},{32,48},{48,64},{64,80},{80,96},{96,112},{112,128},... | collective-permute-start | bytes 24584 | tf_op jit(solution)/shard_map/while/body/eval_jaxpr/ppermute | solution.py:15
  209.4 18.2 %collective-permute-start.4 = (f32[32,512]{1,0:T(8,128)S(1)}, f32[32,512]{1,0:T(8,128)S(1)}, u32[]{:S(2)}, u32[]{:S(2)}) collective-permute-start(f32[32,512]{1,0:T(8,128)S(1)} %broadcast_select_fusion.5), channel_id=1, source_target_pairs={{0,16},{16,32},{32,48},{48,64},{64,80},{80,96},{96,112},{112,128},... | collective-permute-start | bytes 196616 | tf_op jit(solution)/shard_map/while/body/eval_jaxpr/ppermute | solution.py:15
  229.6 17.8 %collective-permute-start.2 = (f32[32]{0:T(128)S(1)}, f32[32]{0:T(128)S(1)}, u32[]{:S(2)}, u32[]{:S(2)}) collective-permute-start(f32[32]{0:T(128)S(1)} %get-tuple-element.271), channel_id=1, source_target_pairs={{0,16},{16,32},{32,48},{48,64},{64,80},{80,96},{96,112},{112,128},... | collective-permute-start | bytes 392 | tf_op jit(solution)/shard_map/while/body/eval_jaxpr/ppermute | solution.py:15
  232.5 27.2 %collective-permute-start.3 = (f32[32,64]{1,0:T(8,128)S(1)}, f32[32,64]{1,0:T(8,128)S(1)}, u32[]{:S(2)}, u32[]{:S(2)}) collective-permute-start(f32[32,64]{1,0:T(8,128)S(1)} %broadcast_select_fusion.4), channel_id=1, source_target_pairs={{0,16},{16,32},{32,48},{48,64},{64,80},{80,96},{96,112},{112,128},... | collective-permute-start | bytes 24584 | tf_op jit(solution)/shard_map/while/body/eval_jaxpr/ppermute | solution.py:15
  242.7 18.1 %collective-permute-start.4 = (f32[32,512]{1,0:T(8,128)S(1)}, f32[32,512]{1,0:T(8,128)S(1)}, u32[]{:S(2)}, u32[]{:S(2)}) collective-permute-start(f32[32,512]{1,0:T(8,128)S(1)} %broadcast_select_fusion.5), channel_id=1, source_target_pairs={{0,16},{16,32},{32,48},{48,64},{64,80},{80,96},{96,112},{112,128},... | collective-permute-start | bytes 196616 | tf_op jit(solution)/shard_map/while/body/eval_jaxpr/ppermute | solution.py:15
  245.5 13.0 %collective-permute-start = (f32[32,512]{1,0:T(8,128)S(1)}, f32[32,512]{1,0:T(8,128)S(1)}, u32[]{:S(2)}, u32[]{:S(2)}) collective-permute-start(f32[32,512]{1,0:T(8,128)S(1)} %get-tuple-element.269), channel_id=1, source_target_pairs={{0,16},{16,32},{32,48},{48,64},{64,80},{80,96},{96,112},{112,128},... | collective-permute-start | bytes 196616 | tf_op jit(solution)/shard_map/while/body/eval_jaxpr/ppermute | solution.py:15
  264.8 21.5 %collective-permute-start.3 = (f32[32,64]{1,0:T(8,128)S(1)}, f32[32,64]{1,0:T(8,128)S(1)}, u32[]{:S(2)}, u32[]{:S(2)}) collective-permute-start(f32[32,64]{1,0:T(8,128)S(1)} %broadcast_select_fusion.4), channel_id=1, source_target_pairs={{0,16},{16,32},{32,48},{48,64},{64,80},{80,96},{96,112},{112,128},... | collective-permute-start | bytes 24584 | tf_op jit(solution)/shard_map/while/body/eval_jaxpr/ppermute | solution.py:15
  268.7 18.8 %collective-permute-start.4 = (f32[32,512]{1,0:T(8,128)S(1)}, f32[32,512]{1,0:T(8,128)S(1)}, u32[]{:S(2)}, u32[]{:S(2)}) collective-permute-start(f32[32,512]{1,0:T(8,128)S(1)} %broadcast_select_fusion.5), channel_id=1, source_target_pairs={{0,16},{16,32},{32,48},{48,64},{64,80},{80,96},{96,112},{112,128},... | collective-permute-start | bytes 196616 | tf_op jit(solution)/shard_map/while/body/eval_jaxpr/ppermute | solution.py:15
  289.5 16.6 %collective-permute-start.2 = (f32[32]{0:T(128)S(1)}, f32[32]{0:T(128)S(1)}, u32[]{:S(2)}, u32[]{:S(2)}) collective-permute-start(f32[32]{0:T(128)S(1)} %get-tuple-element.271), channel_id=1, source_target_pairs={{0,16},{16,32},{32,48},{48,64},{64,80},{80,96},{96,112},{112,128},... | collective-permute-start | bytes 392 | tf_op jit(solution)/shard_map/while/body/eval_jaxpr/ppermute | solution.py:15
  291.5 27.4 %collective-permute-start.3 = (f32[32,64]{1,0:T(8,128)S(1)}, f32[32,64]{1,0:T(8,128)S(1)}, u32[]{:S(2)}, u32[]{:S(2)}) collective-permute-start(f32[32,64]{1,0:T(8,128)S(1)} %broadcast_select_fusion.4), channel_id=1, source_target_pairs={{0,16},{16,32},{32,48},{48,64},{64,80},{80,96},{96,112},{112,128},... | collective-permute-start | bytes 24584 | tf_op jit(solution)/shard_map/while/body/eval_jaxpr/ppermute | solution.py:15
  296.1 24.0 %collective-permute-start.4 = (f32[32,512]{1,0:T(8,128)S(1)}, f32[32,512]{1,0:T(8,128)S(1)}, u32[]{:S(2)}, u32[]{:S(2)}) collective-permute-start(f32[32,512]{1,0:T(8,128)S(1)} %broadcast_select_fusion.5), channel_id=1, source_target_pairs={{0,16},{16,32},{32,48},{48,64},{64,80},{80,96},{96,112},{112,128},... | collective-permute-start | bytes 196616 | tf_op jit(solution)/shard_map/while/body/eval_jaxpr/ppermute | solution.py:15
  304.2 13.5 %collective-permute-start = (f32[32,512]{1,0:T(8,128)S(1)}, f32[32,512]{1,0:T(8,128)S(1)}, u32[]{:S(2)}, u32[]{:S(2)}) collective-permute-start(f32[32,512]{1,0:T(8,128)S(1)} %get-tuple-element.269), channel_id=1, source_target_pairs={{0,16},{16,32},{32,48},{48,64},{64,80},{80,96},{96,112},{112,128},... | collective-permute-start | bytes 196616 | tf_op jit(solution)/shard_map/while/body/eval_jaxpr/ppermute | solution.py:15
  324.1 18.9 %collective-permute-start.3 = (f32[32,64]{1,0:T(8,128)S(1)}, f32[32,64]{1,0:T(8,128)S(1)}, u32[]{:S(2)}, u32[]{:S(2)}) collective-permute-start(f32[32,64]{1,0:T(8,128)S(1)} %broadcast_select_fusion.4), channel_id=1, source_target_pairs={{0,16},{16,32},{32,48},{48,64},{64,80},{80,96},{96,112},{112,128},... | collective-permute-start | bytes 24584 | tf_op jit(solution)/shard_map/while/body/eval_jaxpr/ppermute | solution.py:15
  327.9 16.2 %collective-permute-start.4 = (f32[32,512]{1,0:T(8,128)S(1)}, f32[32,512]{1,0:T(8,128)S(1)}, u32[]{:S(2)}, u32[]{:S(2)}) collective-permute-start(f32[32,512]{1,0:T(8,128)S(1)} %broadcast_select_fusion.5), channel_id=1, source_target_pairs={{0,16},{16,32},{32,48},{48,64},{64,80},{80,96},{96,112},{112,128},... | collective-permute-start | bytes 196616 | tf_op jit(solution)/shard_map/while/body/eval_jaxpr/ppermute | solution.py:15
  346.2 17.0 %collective-permute-start.2 = (f32[32]{0:T(128)S(1)}, f32[32]{0:T(128)S(1)}, u32[]{:S(2)}, u32[]{:S(2)}) collective-permute-start(f32[32]{0:T(128)S(1)} %get-tuple-element.271), channel_id=1, source_target_pairs={{0,16},{16,32},{32,48},{48,64},{64,80},{80,96},{96,112},{112,128},... | collective-permute-start | bytes 392 | tf_op jit(solution)/shard_map/while/body/eval_jaxpr/ppermute | solution.py:15
  348.1 26.9 %collective-permute-start.3 = (f32[32,64]{1,0:T(8,128)S(1)}, f32[32,64]{1,0:T(8,128)S(1)}, u32[]{:S(2)}, u32[]{:S(2)}) collective-permute-start(f32[32,64]{1,0:T(8,128)S(1)} %broadcast_select_fusion.4), channel_id=1, source_target_pairs={{0,16},{16,32},{32,48},{48,64},{64,80},{80,96},{96,112},{112,128},... | collective-permute-start | bytes 24584 | tf_op jit(solution)/shard_map/while/body/eval_jaxpr/ppermute | solution.py:15
  357.0 19.3 %collective-permute-start.4 = (f32[32,512]{1,0:T(8,128)S(1)}, f32[32,512]{1,0:T(8,128)S(1)}, u32[]{:S(2)}, u32[]{:S(2)}) collective-permute-start(f32[32,512]{1,0:T(8,128)S(1)} %broadcast_select_fusion.5), channel_id=1, source_target_pairs={{0,16},{16,32},{32,48},{48,64},{64,80},{80,96},{96,112},{112,128},... | collective-permute-start | bytes 196616 | tf_op jit(solution)/shard_map/while/body/eval_jaxpr/ppermute | solution.py:15
  378.3 15.7 %collective-permute-start.2 = (f32[32]{0:T(128)S(1)}, f32[32]{0:T(128)S(1)}, u32[]{:S(2)}, u32[]{:S(2)}) collective-permute-start(f32[32]{0:T(128)S(1)} %get-tuple-element.271), channel_id=1, source_target_pairs={{0,16},{16,32},{32,48},{48,64},{64,80},{80,96},{96,112},{112,128},... | collective-permute-start | bytes 392 | tf_op jit(solution)/shard_map/while/body/eval_jaxpr/ppermute | solution.py:15
  380.2 27.1 %collective-permute-start.3 = (f32[32,64]{1,0:T(8,128)S(1)}, f32[32,64]{1,0:T(8,128)S(1)}, u32[]{:S(2)}, u32[]{:S(2)}) collective-permute-start(f32[32,64]{1,0:T(8,128)S(1)} %broadcast_select_fusion.4), channel_id=1, source_target_pairs={{0,16},{16,32},{32,48},{48,64},{64,80},{80,96},{96,112},{112,128},... | collective-permute-start | bytes 24584 | tf_op jit(solution)/shard_map/while/body/eval_jaxpr/ppermute | solution.py:15
  384.1 24.5 %collective-permute-start.4 = (f32[32,512]{1,0:T(8,128)S(1)}, f32[32,512]{1,0:T(8,128)S(1)}, u32[]{:S(2)}, u32[]{:S(2)}) collective-permute-start(f32[32,512]{1,0:T(8,128)S(1)} %broadcast_select_fusion.5), channel_id=1, source_target_pairs={{0,16},{16,32},{32,48},{48,64},{64,80},{80,96},{96,112},{112,128},... | collective-permute-start | bytes 196616 | tf_op jit(solution)/shard_map/while/body/eval_jaxpr/ppermute | solution.py:15
  392.1 14.2 %collective-permute-start = (f32[32,512]{1,0:T(8,128)S(1)}, f32[32,512]{1,0:T(8,128)S(1)}, u32[]{:S(2)}, u32[]{:S(2)}) collective-permute-start(f32[32,512]{1,0:T(8,128)S(1)} %get-tuple-element.269), channel_id=1, source_target_pairs={{0,16},{16,32},{32,48},{48,64},{64,80},{80,96},{96,112},{112,128},... | collective-permute-start | bytes 196616 | tf_op jit(solution)/shard_map/while/body/eval_jaxpr/ppermute | solution.py:15
  412.5 19.0 %collective-permute-start.3 = (f32[32,64]{1,0:T(8,128)S(1)}, f32[32,64]{1,0:T(8,128)S(1)}, u32[]{:S(2)}, u32[]{:S(2)}) collective-permute-start(f32[32,64]{1,0:T(8,128)S(1)} %broadcast_select_fusion.4), channel_id=1, source_target_pairs={{0,16},{16,32},{32,48},{48,64},{64,80},{80,96},{96,112},{112,128},... | collective-permute-start | bytes 24584 | tf_op jit(solution)/shard_map/while/body/eval_jaxpr/ppermute | solution.py:15
  416.4 16.4 %collective-permute-start.4 = (f32[32,512]{1,0:T(8,128)S(1)}, f32[32,512]{1,0:T(8,128)S(1)}, u32[]{:S(2)}, u32[]{:S(2)}) collective-permute-start(f32[32,512]{1,0:T(8,128)S(1)} %broadcast_select_fusion.5), channel_id=1, source_target_pairs={{0,16},{16,32},{32,48},{48,64},{64,80},{80,96},{96,112},{112,128},... | collective-permute-start | bytes 196616 | tf_op jit(solution)/shard_map/while/body/eval_jaxpr/ppermute | solution.py:15
  434.8 15.0 %collective-permute-start.2 = (f32[32]{0:T(128)S(1)}, f32[32]{0:T(128)S(1)}, u32[]{:S(2)}, u32[]{:S(2)}) collective-permute-start(f32[32]{0:T(128)S(1)} %get-tuple-element.271), channel_id=1, source_target_pairs={{0,16},{16,32},{32,48},{48,64},{64,80},{80,96},{96,112},{112,128},... | collective-permute-start | bytes 392 | tf_op jit(solution)/shard_map/while/body/eval_jaxpr/ppermute | solution.py:15
  436.7 20.8 %collective-permute-start.3 = (f32[32,64]{1,0:T(8,128)S(1)}, f32[32,64]{1,0:T(8,128)S(1)}, u32[]{:S(2)}, u32[]{:S(2)}) collective-permute-start(f32[32,64]{1,0:T(8,128)S(1)} %broadcast_select_fusion.4), channel_id=1, source_target_pairs={{0,16},{16,32},{32,48},{48,64},{64,80},{80,96},{96,112},{112,128},... | collective-permute-start | bytes 24584 | tf_op jit(solution)/shard_map/while/body/eval_jaxpr/ppermute | solution.py:15
  440.6 18.2 %collective-permute-start.4 = (f32[32,512]{1,0:T(8,128)S(1)}, f32[32,512]{1,0:T(8,128)S(1)}, u32[]{:S(2)}, u32[]{:S(2)}) collective-permute-start(f32[32,512]{1,0:T(8,128)S(1)} %broadcast_select_fusion.5), channel_id=1, source_target_pairs={{0,16},{16,32},{32,48},{48,64},{64,80},{80,96},{96,112},{112,128},... | collective-permute-start | bytes 196616 | tf_op jit(solution)/shard_map/while/body/eval_jaxpr/ppermute | solution.py:15
  460.8 18.8 %collective-permute-start.2 = (f32[32]{0:T(128)S(1)}, f32[32]{0:T(128)S(1)}, u32[]{:S(2)}, u32[]{:S(2)}) collective-permute-start(f32[32]{0:T(128)S(1)} %get-tuple-element.271), channel_id=1, source_target_pairs={{0,16},{16,32},{32,48},{48,64},{64,80},{80,96},{96,112},{112,128},... | collective-permute-start | bytes 392 | tf_op jit(solution)/shard_map/while/body/eval_jaxpr/ppermute | solution.py:15
  465.5 25.7 %collective-permute-start.3 = (f32[32,64]{1,0:T(8,128)S(1)}, f32[32,64]{1,0:T(8,128)S(1)}, u32[]{:S(2)}, u32[]{:S(2)}) collective-permute-start(f32[32,64]{1,0:T(8,128)S(1)} %broadcast_select_fusion.4), channel_id=1, source_target_pairs={{0,16},{16,32},{32,48},{48,64},{64,80},{80,96},{96,112},{112,128},... | collective-permute-start | bytes 24584 | tf_op jit(solution)/shard_map/while/body/eval_jaxpr/ppermute | solution.py:15
  475.8 16.7 %collective-permute-start.4 = (f32[32,512]{1,0:T(8,128)S(1)}, f32[32,512]{1,0:T(8,128)S(1)}, u32[]{:S(2)}, u32[]{:S(2)}) collective-permute-start(f32[32,512]{1,0:T(8,128)S(1)} %broadcast_select_fusion.5), channel_id=1, source_target_pairs={{0,16},{16,32},{32,48},{48,64},{64,80},{80,96},{96,112},{112,128},... | collective-permute-start | bytes 196616 | tf_op jit(solution)/shard_map/while/body/eval_jaxpr/ppermute | solution.py:15
  496.4 15.8 %collective-permute-start.5 = (f32[32]{0:T(128)S(1)}, f32[32]{0:T(128)S(1)}, u32[]{:S(2)}, u32[]{:S(2)}) collective-permute-start(f32[32]{0:T(128)S(1)} %get-tuple-element.66), channel_id=1, source_target_pairs={{0,16},{16,32},{32,48},{48,64},{64,80},{80,96},{96,112},{112,128},... | collective-permute-start | bytes 392 | tf_op jit(solution)/shard_map/ppermute | solution.py:15
  517.9 55.2 %all-to-all-start.1 = ((f32[16,32,576]{2,1,0:T(8,128)}), f32[16,32,576]{2,1,0:T(8,128)S(1)}, u32[]{:S(2)}, u32[]{:S(2)}) async-start(f32[16,32,576]{2,1,0:T(8,128)} %bitcast.2), calls=%async_computation.1 | async-start | bytes 2621440 | tf_op jit(solution)/shard_map/all_to_all | solution.py:55
  527.5 28.3 %collective-permute-start.10 = (f32[32,512]{1,0:T(8,128)S(1)}, f32[32,512]{1,0:T(8,128)S(1)}, u32[]{:S(2)}, u32[]{:S(2)}) collective-permute-start(f32[32,512]{1,0:T(8,128)S(1)} %get-tuple-element.71), channel_id=1, source_target_pairs={{0,16},{16,32},{32,48},{48,64},{64,80},{80,96},{96,112},{112,128},... | collective-permute-start | bytes 196616 | tf_op jit(solution)/shard_map/ppermute | solution.py:15
  555.8 17.4 %collective-permute-start.11 = (f32[32,512]{1,0:T(8,128)S(1)}, f32[32,512]{1,0:T(8,128)S(1)}, u32[]{:S(2)}, u32[]{:S(2)}) collective-permute-start(f32[32,512]{1,0:T(8,128)S(1)} %collective-permute-done.10), channel_id=1, source_target_pairs={{0,256},{16,272},{32,288},{48,304},{64,320},{80,336},{96,352},{112... | collective-permute-start | bytes 196616 | tf_op jit(solution)/shard_map/ppermute | solution.py:15
  (39 other events, 432.4 us)
where the time goes:
time: 582 us; the launch traced here: 579 us
  starting transfers between devices  261 us (45%)
  waiting for transfers between devices  231 us (40%)
  matrix products  74 us (13%)
    ppermute x82, starting transfers between devices, passed_along(): lax.ppermute(value, axis, [(i, (i + by) % length) for i in range(length)])  243 us
    ppermute x82, waiting for transfers between devices, passed_along(): lax.ppermute(value, axis, [(i, (i + by) % length) for i in range(length)])  196 us
    all_to_all x1, waiting for transfers between devices, from_everyone(): lax.all_to_all(jnp.broadcast_to(value[None], (length, *value.shape)), axi...  34.8 us
    dot_general x17, matrix products, resident_side(): jnp.dot(weight, away_scaled, precision=HIGH, preferred_element_type=jnp.f...  23.7 us
    dot_general x17, matrix products, pair_terms(): lax.dot_general(home_scaled, away_scaled, ROWS_RULE, precision=HIGH, pref...  19.4 us
  transfers between devices with their start and end apart: 84, of which 36 were waited for; matrix products, arithmetic and copies ran while one was open for 7% of the time, Pallas kernels for 0%

commit v1 on v0

v1 whole, which is shorter than its diff:
```python
import functools

import jax
import jax.numpy as jnp
from jax import lax
from jax.experimental import pallas as pl
from jax.experimental.pallas import tpu as pltpu
from jax.sharding import PartitionSpec as P

BF = jnp.bfloat16
F32 = jnp.float32
NT = (((1,), (1,)), ((), ()))
NN = (((1,), (0,)), ((), ()))
MESH = pl.DeviceIdType.MESH

OWN = 32
W = 640
CHIPS_Z = 16
PLANE = 4


def place():
    blk, sub = lax.axis_index("blk"), lax.axis_index("sub")
    core = lax.rem(blk, 2)
    z = lax.rem(lax.div(blk, 2), 4) * 4 + lax.div(sub, 4)
    y = lax.div(blk, 8)
    x = lax.rem(sub, 4)
    return x, y, z, core


def device(x, y, z, core):
    return (y * 8 + lax.div(z, 4) * 2 + core, lax.rem(z, 4) * 4 + x)


def peers():
    x, y, z, core = place()
    along_x = [None] + [device(lax.rem(x + k, 4), y, z, core) for k in (1, 2, 3)]
    along_y = [None] + [device(x, lax.rem(y + k, 4), z, core) for k in (1, 2, 3)]
    up = device(x, y, lax.rem(z + 1, CHIPS_Z), core)
    down = device(x, y, lax.rem(z + CHIPS_Z - 1, CHIPS_Z), core)
    partner = device(x, y, z, 1 - core)
    return along_x, along_y, up, down, partner


def meet(devices):
    barrier = pltpu.get_barrier_semaphore()
    for d in devices:
        pl.semaphore_signal(barrier, inc=1, device_id=d, device_id_type=MESH)
    pl.semaphore_wait(barrier, len(devices))


def copy_to(src, dst, send, recv, to):
    return pltpu.make_async_remote_copy(
        src_ref=src, dst_ref=dst, send_sem=send, recv_sem=recv, device_id=to, device_id_type=MESH
    )


def gather_kernel(f_ref, ls_ref, pr_ref, ct_ref, rows_ref, line_ref, zs, zr, ks, kr, as_, ar, bs, br):
    along_x, along_y, up, down, partner = peers()
    own = f_ref[...] / ls_ref[...]
    line_ref[0, 0, :, 0:512] = own
    line_ref[0, 0, :, 512:576] = pr_ref[...]
    line_ref[0, 0, :, 576:640] = ct_ref[...]
    for h in range(2):
        part = slice(h * 16, h * 16 + 16)
        rows_ref[h, 0, 0, :, 0:512] = own[part]
        rows_ref[h, 0, 0, :, 512:576] = pr_ref[part, :]
        rows_ref[h, 0, 0, :, 576:640] = ct_ref[part, :]
    meet(along_x[1:] + along_y[1:] + [up, down, partner])

    def z_copy(way, s, q):
        src = s if way == 0 else (CHIPS_Z - s if not isinstance(s, int) or s else 0)
        dst = s + 1 if way == 0 else CHIPS_Z - 1 - s
        rows = pl.ds(8 * q, 8)
        return copy_to(
            line_ref.at[0, src, rows], line_ref.at[0, dst, rows],
            zs.at[way, s, q], zr.at[way, s, q], (up, down)[way],
        )

    def k_copy(slot):
        return copy_to(line_ref.at[0, slot], line_ref.at[1, slot], ks.at[slot], kr.at[slot], partner)

    def a_first(k):
        return copy_to(rows_ref.at[0, 0, 0], rows_ref.at[0, 0, 4 - k], as_.at[0, k], ar.at[0, k], along_x[k])

    def a_then(dx, k):
        return copy_to(rows_ref.at[0, 0, dx], rows_ref.at[0, 4 - k, dx], as_.at[1 + dx, k], ar.at[1 + dx, k], along_y[k])

    def b_first(k):
        return copy_to(rows_ref.at[1, 0, 0], rows_ref.at[1, 4 - k, 0], bs.at[0, k], br.at[0, k], along_y[k])

    def b_then(dy, k):
        return copy_to(rows_ref.at[1, dy, 0], rows_ref.at[1, dy, 4 - k], bs.at[1 + dy, k], br.at[1 + dy, k], along_x[k])

    for q in range(4):
        z_copy(0, 0, q).start()
        z_copy(1, 0, q).start()
    for k in (1, 3, 2):
        a_first(k).start()
        b_first(k).start()
    k_copy(0).start()
    for k in (1, 3, 2):
        a_then(0, k).start()
        b_then(0, k).start()

    def z_step(s):
        for q in range(4):
            for way in range(2):
                z_copy(way, s - 1, q).wait_recv()
                z_copy(way, s, q).start()
        k_copy(s).start()
        k_copy(CHIPS_Z - s).start()

    z_step(1)
    for k in (1, 3, 2):
        a_first(k).wait_recv()
        for j in (1, 3, 2):
            a_then(4 - k, j).start()
        b_first(k).wait_recv()
        for j in (1, 3, 2):
            b_then(4 - k, j).start()

    def body(s, carry):
        z_step(s)
        return carry

    lax.fori_loop(2, 7, body, 0)
    for q in range(4):
        for way in range(2):
            z_copy(way, 6, q).wait_recv()
            if q // 2 == way:
                z_copy(way, 7, q).start()
    k_copy(7).start()
    k_copy(9).start()
    for way in range(2):
        for q in (2 * way, 2 * way + 1):
            z_copy(way, 7, q).wait_recv()
    k_copy(8).start()

    for dx in range(4):
        for k in (1, 2, 3):
            a_then(dx, k).wait_recv()
            b_then(dx, k).wait_recv()
    for slot in range(16):
        k_copy(slot).wait()
    for k in (1, 2, 3):
        a_first(k).wait_send()
        b_first(k).wait_send()
        for dx in range(4):
            a_then(dx, k).wait_send()
            b_then(dx, k).wait_send()

    def drain(s, carry):
        for q in range(4):
            for way in range(2):
                z_copy(way, s, q).wait_send()
        return carry

    for q in range(4):
        for way in range(2):
            z_copy(way, 0, q).wait_send()
    lax.fori_loop(1, 7, drain, 0)
    for way in range(2):
        for q in (2 * way, 2 * way + 1):
            z_copy(way, 7, q).wait_send()


def halves(x):
    high = x.astype(BF)
    return high, (x - high.astype(F32)).astype(BF)


def dot(a, b, dims):
    return lax.dot_general(a, b, dims, preferred_element_type=F32)


COLS = 256
ROWS = 512


def pair_kernel(rows_ref, line_ref, out_ref, row_parts, pair_parts, row_norms, col_parts, swapped, col_stack, probe_stack):
    n_rows = rows_ref.shape[0]
    n_cols = line_ref.shape[0]

    def prepare(r, carry):
        rows = pl.ds(pl.multiple_of(r * 128, 128), 128)
        x = rows_ref[rows, 0:512]
        high, low = halves(x)
        row_parts[0, rows, :] = high
        row_parts[1, rows, :] = low
        row_norms[rows, :] = jnp.broadcast_to(0.5 * jnp.sum(x * x, axis=1, keepdims=True), (128, 128))
        high, low = halves(rows_ref[rows, 512:640])
        pair_parts[rows, 0:128] = high
        pair_parts[rows, 128:256] = low
        out_ref[rows, :] = jnp.zeros((128, W), F32)
        return carry

    lax.fori_loop(0, n_rows // 128, prepare, 0)

    def chunk(c, carry):
        cols = pl.ds(pl.multiple_of(c * COLS, COLS), COLS)
        x = line_ref[cols, 0:512]
        high, low = halves(x)
        col_parts[0:COLS, :] = high
        col_parts[COLS : 2 * COLS, :] = low
        square = x * x
        folded = square[:, 0:128] + square[:, 128:256] + square[:, 256:384] + square[:, 384:512]
        col_norms = 0.5 * jnp.sum(folded.T, axis=0, keepdims=True)
        pr_high, pr_low = halves(line_ref[cols, 512:576])
        ct_high, ct_low = halves(line_ref[cols, 576:640])
        for k, (ct, pr) in enumerate(((ct_high, pr_high), (ct_low, pr_low))):
            for at in (0, 128):
                swapped[k * COLS : (k + 1) * COLS, at : at + 64] = ct
                swapped[k * COLS : (k + 1) * COLS, at + 64 : at + 128] = pr
        for k, part in enumerate((high, high, low)):
            col_stack[k * COLS : (k + 1) * COLS, :] = part
        for k in range(2):
            probe_stack[k * COLS : (k + 1) * COLS, 0:64] = pr_high
            probe_stack[k * COLS : (k + 1) * COLS, 64:128] = pr_low

        def block(r, carry):
            rows = pl.ds(pl.multiple_of(r * ROWS, ROWS), ROWS)
            both = col_parts[...]
            a = dot(row_parts[0, rows, :], both, NT) + dot(row_parts[1, rows, :], both, NT)
            inner = a[:, 0:COLS] + a[:, COLS : 2 * COLS]
            b = dot(pair_parts[rows, :], swapped[...], NT)
            cross = b[:, 0:COLS] + b[:, COLS : 2 * COLS]
            norms = row_norms[rows, :]
            norms = jnp.concatenate([norms] * (COLS // 128), axis=1)
            kernel = jnp.exp(inner - norms - col_norms)
            weight = kernel * cross
            k_high, k_low = halves(kernel)
            w_high, w_low = halves(weight)
            gradient = dot(jnp.concatenate([w_high, w_low, w_high], axis=1), col_stack[...], NN)
            product = dot(jnp.concatenate([k_high, k_low], axis=1), probe_stack[...], NN)
            out_ref[rows, 0:512] += gradient
            sums = jnp.sum(weight, axis=1, keepdims=True)
            out_ref[rows, 512:640] += jnp.concatenate(
                [product[:, 0:64] + product[:, 64:128], jnp.broadcast_to(sums, (ROWS, 64))], axis=1
            )
            return carry

        lax.fori_loop(0, n_rows // ROWS, block, 0)
        return carry

    lax.fori_loop(0, n_cols // COLS, chunk, 0)


def scatter_kernel(part_ref, f_ref, ls_ref, product_ref, gradient_ref, a1, b1, at, bt, a2, b2, ss, sr):
    along_x, along_y, _, _, _ = peers()
    meet(along_x[1:] + along_y[1:])

    def a_first(k):
        return copy_to(part_ref.at[0, :, k], a1.at[k - 1], ss.at[0, k], sr.at[0, k], along_x[k])

    def b_first(k):
        return copy_to(part_ref.at[1, k], b1.at[k - 1], ss.at[1, k], sr.at[1, k], along_y[k])

    def a_then(k):
        return copy_to(at.at[k], a2.at[k - 1], ss.at[2, k], sr.at[2, k], along_y[k])

    def b_then(k):
        return copy_to(bt.at[k], b2.at[k - 1], ss.at[3, k], sr.at[3, k], along_x[k])

    for k in (1, 3, 2):
        a_first(k).start()
        b_first(k).start()
    for k in (1, 2, 3):
        a_first(k).wait_recv()
        b_first(k).wait_recv()
    for j in (1, 3, 2, 0):
        at[j] = part_ref[0, j, 0] + a1[0, j] + a1[1, j] + a1[2, j]
        bt[j] = part_ref[1, 0, j] + b1[0, j] + b1[1, j] + b1[2, j]
        if j:
            a_then(j).start()
            b_then(j).start()
    for k in (1, 2, 3):
        a_then(k).wait_recv()
        b_then(k).wait_recv()
    for h, (t, u) in enumerate(((at, a2), (bt, b2))):
        rows = slice(16 * h, 16 * h + 16)
        total = t[0] + u[0] + u[1] + u[2]
        scaled = f_ref[rows, :] / ls_ref[...]
        product_ref[rows, :] = total[:, 512:576]
        gradient_ref[rows, :] = total[:, 0:512] - total[:, 576:577] * scaled
    for k in (1, 2, 3):
        for c in (a_first, b_first, a_then, b_then):
            c(k).wait_send()


VMEM = pl.BlockSpec(memory_space=pltpu.VMEM)
DMA = pltpu.SemaphoreType.DMA


def on_device(features, lengthscale, probes, cotangent):
    scale = lengthscale[None, :]
    rows, line = pl.pallas_call(
        gather_kernel,
        out_shape=(
            jax.ShapeDtypeStruct((2, 4, 4, 16, W), F32),
            jax.ShapeDtypeStruct((2, 16, OWN, W), F32),
        ),
        in_specs=[VMEM] * 4,
        out_specs=(VMEM, VMEM),
        scratch_shapes=[
            DMA((2, 8, 4)), DMA((2, 8, 4)), DMA((16,)), DMA((16,)),
            DMA((5, 4)), DMA((5, 4)), DMA((5, 4)), DMA((5, 4)),
        ],
        compiler_params=pltpu.CompilerParams(collective_id=0, has_side_effects=True),
        name="gather",
    )(features, scale, probes, cotangent)
    part = pl.pallas_call(
        pair_kernel,
        out_shape=jax.ShapeDtypeStruct((512, W), F32),
        in_specs=[VMEM] * 2,
        out_specs=VMEM,
        scratch_shapes=[
            pltpu.VMEM((2, 512, 512), BF), pltpu.VMEM((512, 256), BF), pltpu.VMEM((512, 128), F32),
            pltpu.VMEM((2 * COLS, 512), BF), pltpu.VMEM((2 * COLS, 256), BF),
            pltpu.VMEM((3 * COLS, 512), BF), pltpu.VMEM((2 * COLS, 128), BF),
        ],
        name="pairs",
    )(rows.reshape(512, W), line.reshape(1024, W))
    return pl.pallas_call(
        scatter_kernel,
        out_shape=(jax.ShapeDtypeStruct(probes.shape, F32), jax.ShapeDtypeStruct(features.shape, F32)),
        in_specs=[VMEM] * 3,
        out_specs=(VMEM, VMEM),
        scratch_shapes=[
            pltpu.VMEM((3, 4, 16, W), F32), pltpu.VMEM((3, 4, 16, W), F32),
            pltpu.VMEM((4, 16, W), F32), pltpu.VMEM((4, 16, W), F32),
            pltpu.VMEM((3, 16, W), F32), pltpu.VMEM((3, 16, W), F32),
            DMA((4, 4)), DMA((4, 4)),
        ],
        compiler_params=pltpu.CompilerParams(collective_id=1, has_side_effects=True),
        name="scatter",
    )(part.reshape(2, 4, 4, 16, W), features, scale)


def solution(mesh):
    spec = P(("blk", "sub"), None)
    return jax.shard_map(
        on_device, mesh=mesh, in_specs=(spec, P(), spec, spec), out_specs=(spec, spec), check_vma=False
    )
```

time: 582 us -> 79.2 us (0.14)
  the two profiles are of different devices: /device:TPU:34 before, /device:TPU:1 now
where the time goes in v1:
time: 79.2 us; the launch traced here: 78.9 us
  Pallas kernels  75.4 us (95%)
  local copies, waits for them, and re-layouts  2.8 us (4%)
    pallas_call x1, Pallas kernels, on_device(): pl.pallas_call(gather_kernel, out_shape=(jax.ShapeDtypeStruct((2, 4, 4, 1...  45.2 us
    pallas_call x1, Pallas kernels, on_device(): pl.pallas_call(scatter_kernel, out_shape=(jax.ShapeDtypeStruct(probes.sha...  18.3 us
    pallas_call x1, Pallas kernels, on_device(): pl.pallas_call(pair_kernel, out_shape=jax.ShapeDtypeStruct((512, W), F32)...  11.9 us
    unnamed x2, local copies, waits for them, and re-layouts  2.8 us

profile of v1, /device:TPU:1, one launch (start us, length us, event | category | flops | bytes accessed | tf_op | source)
XLA Modules:
  0.0 78.9 jit_solution(12016153077974106946)
XLA Ops:
  0.6 45.2 %gather.1 = (f32[2,4,4,16,640]{4,3,2,1,0:T(8,128)}, f32[2,16,32,640]{3,2,1,0:T(8,128)}) custom-call(f32[32,512]{1,0:T(8,128)} %f_ref.3, f32[1,512]{1,0:T(1,128)} %bitcast.7, f32[32,64]{1,0:T(8,128)} %pr_ref.1, f32[32,64]{1,0:T(8,128)} %ct_ref.1), custom_call_target="tpu_custom_call" | custom-call | tf_op jit(solution)/shard_map/gather/pallas_call | solution.py:297
  45.8 11.9 %pairs.1 = f32[512,640]{1,0:T(8,128)} custom-call(f32[512,640]{1,0:T(8,128)} %bitcast.6, f32[1024,640]{1,0:T(8,128)} %bitcast.5), custom_call_target="tpu_custom_call" | custom-call | tf_op jit(solution)/shard_map/pairs/pallas_call | solution.py:312
  57.8 18.3 %scatter.1 = (f32[32,64]{1,0:T(8,128)}, f32[32,512]{1,0:T(8,128)}) custom-call(f32[2,4,4,16,640]{4,3,2,1,0:T(8,128)} %bitcast.4, f32[32,512]{1,0:T(8,128)} %f_ref.3, f32[1,512]{1,0:T(1,128)} %bitcast.8), custom_call_target="tpu_custom_call" | custom-call | tf_op jit(solution)/shard_map/scatter/pallas_call | solution.py:324
  76.1 1.3 %copy.8 = f32[32,64]{1,0:T(8,128)} copy(f32[32,64]{1,0:T(8,128)} %get-tuple-element.8) | data formatting | bytes 16384
  77.4 1.5 %copy.9 = f32[32,512]{1,0:T(8,128)} copy(f32[32,512]{1,0:T(8,128)} %get-tuple-element.9) | data formatting | bytes 131072
